TPU v7x, 256 devices: a whole 4x4x8 slice. The times are simulated.
256 devices in a mesh: dp: 32 (over y_hi, z, core), head: 8 (over x, y_lo).
Axes of the slice: x: 4, y: 4 (y_hi: 2, y_lo: 2; y = y_hi * 2 + y_lo), z: 8, core: 2. Of those that a mesh axis runs over, the one named last changes fastest.
Arguments:
- queries: bfloat16 [24576, 8192], P(('dp', 'head')), may hold values from -6 to 6, as said below
- key_states: bfloat16 [24576, 1024], P(('dp', 'head')), may hold values from -6 to 6, as said below
- value_states: bfloat16 [24576, 1024], P(('dp', 'head')), may hold values from -6 to 6
- document_lengths: int32 [8], replicated, may hold values from 1 to 12288, 24576 in all
Outputs:
- attended: bfloat16 [24576, 8192], P(('dp', 'head'))
Inputs may be any that keep to these rules, and one draw needn't show every extreme that they name: `queries`: within this range. `key_states`: this range. `document_lengths`: the lengths sum to 24576 and the largest is exactly 12288.
All inputs are finite; a program needn't handle non-finite values.
Results may differ from a plain program's by a relative error of at most 0.008.
Values may be sent and summed in bfloat16 or wider, within the bound.
A program may use at most 128 MiB of HBM per device.

v0:
```python
import jax
import jax.numpy as jnp
from jax import lax
from jax.sharding import PartitionSpec as P

HQ = 64
HK = 8
DH = 128
NEGATIVE = -1e30


def document_starts(document_lengths, positions):
    document_ends = jnp.cumsum(document_lengths)
    return jnp.sum(
        jnp.where(document_ends[None, :] <= positions[:, None], document_lengths[None, :], 0),
        axis=1,
    )


def attend_block(state, query_set, key_block, value_block, key_first):
    maxima, totals, accumulated = state
    query_rows, query_positions, query_starts = query_set
    key_positions = key_first + jnp.arange(key_block.shape[0], dtype=jnp.int32)
    allowed = (key_positions[None, :] <= query_positions[:, None]) & (
        key_positions[None, :] >= query_starts[:, None]
    )
    score_scale = query_rows.shape[-1] ** (-0.5)
    scores = (
        jnp.einsum("qhgd,khd->qhgk", query_rows, key_block, preferred_element_type=jnp.float32)
        * score_scale
    )
    scores = jnp.where(allowed[:, None, None, :], scores, NEGATIVE)
    new_maxima = jnp.maximum(maxima, jnp.max(scores, axis=3))
    weights = jnp.where(allowed[:, None, None, :], jnp.exp(scores - new_maxima[..., None]), 0.0)
    factor = jnp.exp(maxima - new_maxima)
    totals = totals * factor + jnp.sum(weights, axis=3)
    accumulated = accumulated * factor[..., None] + jnp.einsum(
        "qhgk,khd->qhgd",
        weights.astype(jnp.bfloat16),
        value_block,
        preferred_element_type=jnp.float32,
    )
    return (new_maxima, totals, accumulated)


def visit(state, query_set, key_block, value_block, key_first):
    block_width = key_block.shape[0]
    latest = jnp.max(query_set[1])
    earliest = jnp.min(query_set[2])
    needed = (key_first >= 0) & (key_first <= latest) & (key_first + block_width - 1 >= earliest)
    return lax.cond(
        needed,
        lambda current: attend_block(current, query_set, key_block, value_block, key_first),
        lambda current: current,
        state,
    )


def on_device(queries, key_states, value_states, document_lengths):
    query_cols, key_cols, value_cols = (
        lax.all_to_all(queries, "head", split_axis=1, concat_axis=0, tiled=True),
        lax.all_to_all(key_states, "head", split_axis=1, concat_axis=0, tiled=True),
        lax.all_to_all(value_states, "head", split_axis=1, concat_axis=0, tiled=True),
    )
    shard_rows = query_cols.shape[0]
    local_kv = key_cols.shape[1] // DH
    group_heads = HQ // HK
    own_queries = query_cols.reshape(shard_rows, local_kv, group_heads, DH)
    key_heads = key_cols.reshape(shard_rows, local_kv, DH)
    value_heads = value_cols.reshape(shard_rows, local_kv, DH)
    dp_index = lax.axis_index("dp")
    offsets = jnp.arange(shard_rows, dtype=jnp.int32)
    own_positions = dp_index * shard_rows + offsets
    query_set = (own_queries, own_positions, document_starts(document_lengths, own_positions))
    set_rows = own_queries.shape[0]
    state = (
        jnp.full((set_rows, local_kv, group_heads), NEGATIVE, jnp.float32),
        jnp.zeros((set_rows, local_kv, group_heads), jnp.float32),
        jnp.zeros((set_rows, local_kv, group_heads, DH), jnp.float32),
    )
    key_piece = lax.all_gather(key_heads, "dp", axis=0, tiled=True)
    value_piece = lax.all_gather(value_heads, "dp", axis=0, tiled=True)
    block_width = min(shard_rows, key_piece.shape[0])

    def fold_step(number, inner_state):
        first_row = number * block_width
        key_block = lax.dynamic_slice_in_dim(key_piece, first_row, block_width, 0)
        value_block = lax.dynamic_slice_in_dim(value_piece, first_row, block_width, 0)
        return visit(inner_state, query_set, key_block, value_block, first_row)

    state = lax.fori_loop(0, key_piece.shape[0] // block_width, fold_step, state)
    own_state = tuple((member for member in state))
    maxima, totals, accumulated = own_state
    attended = (
        (accumulated / totals[..., None])
        .reshape(shard_rows, local_kv * group_heads * DH)
        .astype(jnp.bfloat16)
    )
    return lax.all_to_all(attended, "head", split_axis=0, concat_axis=1, tiled=True)


def solution(mesh):
    placed = (P(("dp", "head"), None), P(("dp", "head"), None), P(("dp", "head"), None), P())
    return jax.shard_map(
        on_device, mesh=mesh, in_specs=placed, out_specs=P(("dp", "head"), None), check_vma=False
    )
```

profile of v0, /device:TPU:144, one launch (start us, length us, event | category | flops | bytes accessed | tf_op | source)
XLA Modules:
  0.0 796.3 jit_solution(5520444923015914160)
XLA Ops:
  7.5 11.6 %all_to_all.64 = bf16[96,8,128]{2,0,1:T(8,128)(2,1)} all-to-all(bf16[96,8,128]{2,0,1:T(8,128)(2,1)S(1)} %copy_bitcast_fusion.1), channel_id=1, replica_groups=mesh['dp'=32,'head'=8] {'head'}, dimensions={1} | all-to-all | bytes 393216 | tf_op jit(solution)/shard_map/all_to_all | solution.py:63
  20.1 9.7 %all_to_all.65 = bf16[96,8,128]{2,0,1:T(8,128)(2,1)} all-to-all(bf16[96,8,128]{2,0,1:T(8,128)(2,1)S(1)} %copy_bitcast_fusion.2), channel_id=1, replica_groups=mesh['dp'=32,'head'=8] {'head'}, dimensions={1} | all-to-all | bytes 393216 | tf_op jit(solution)/shard_map/all_to_all | solution.py:62
  37.8 18.5 %all-to-all-done.1 = bf16[96,8,1024]{2,0,1:T(8,128)(2,1)S(1)} async-done(((bf16[96,8,1024]{2,0,1:T(8,128)(2,1)}), bf16[96,8,1024]{2,0,1:T(8,128)(2,1)S(1)}, u32[]{:S(2)}, u32[]{:S(2)}) %all-to-all-start.1) | async-done | bytes 1572896 | tf_op jit(solution)/shard_map/all_to_all | solution.py:61
  57.0 60.0 %all-gather.5.cloned.1.call-done = bf16[24576,1,128]{2,0,1:T(8,128)(2,1)} async-done(((bf16[768,1,128]{2,0,1:T(8,128)(2,1)}), bf16[24576,1,128]{2,0,1:T(8,128)(2,1)}) %all-gather.5.cloned.1.call-update) | async-done | bytes 6291472 | tf_op jit(solution)/shard_map/all_gather | solution.py:82
  117.0 8.7 %copy.36 = bf16[24576,1,128]{0,2,1:T(8,128)(2,1)} copy(bf16[24576,1,128]{2,0,1:T(8,128)(2,1)} %all-gather.5.cloned.1.call-done) | data formatting | bytes 12582912
  125.6 84.5 %all-gather.3.cloned.1.call-done = bf16[24576,1,128]{2,0,1:T(8,128)(2,1)} async-done(((bf16[768,1,128]{2,0,1:T(8,128)(2,1)}), bf16[24576,1,128]{2,0,1:T(8,128)(2,1)}) %all-gather.3.cloned.1.call-update) | async-done | bytes 6291472 | tf_op jit(solution)/shard_map/all_gather | solution.py:81
  212.1 552.5 %while.22 = (s32[]{:T(128)}, f32[768,1,8]{0,2,1:T(8,128)S(1)}, f32[768,1,8]{0,2,1:T(8,128)S(1)}, f32[768,1,8,128]{0,3,2,1:T(8,128)}, s32[]{:T(128)}, /*index=5*/...) while((s32[]{:T(128)}, f32[768,1,8]{0,2,1:T(8,128)S(1)}, ...), condition=%wide.region_9.10_spmd.clone, body=%wide.region_4.9_spmd.clone.sunk | while | flops 2480623104 | bytes 143152528 | solution.py:91
  223.3 30.2 %conditional.3 = ((f32[768,1,8]{0,2,1:T(8,128)S(1)}, f32[768,1,8]{0,2,1:T(8,128)S(1)}, f32[768,1,8,128]{0,3,2,1:T(8,128)})) conditional(s32[]{:T(128)} %convert_element_type.37, (f32[768,1,8]{0,2,1:T(8,128)S(1)}, f32[768,1,8]{0,2,1:T(8,128)S(1)}, f32[768,1,8,128]{0,3,2,1:T(8,128)}) %tuple.77, (s32[]{:T(128)}, s32[]{:T(128)}, s32[768]{0:T(1024)S(1)}, ...), branch_computations={%region_5.5_spmd, %region_6.8_spmd} | conditional | flops 2480623104 | bytes 143149152 | solution.py:51
  242.5 10.9 %fusion.4 = f32[768,8]{0,1:T(8,128)S(1)} fusion(f32[768,768,8]{1,0,2:T(8,128)} %copy-done.1, f32[768,8]{0,1:T(8,128)S(1)} %bitcast.86, pred[768,768]{0,1:T(8,128)(4,1)S(1)} %compare_and_fusion), kind=kLoop, calls=%fused_computation.5 | loop fusion | flops 23586816 | bytes 19513344 | tf_op jit(solution)/shard_map/while/body/eval_jaxpr/cond/branch_1_fun/reduce_sum | solution.py:36
  254.7 30.2 %conditional.3 = ((f32[768,1,8]{0,2,1:T(8,128)S(1)}, f32[768,1,8]{0,2,1:T(8,128)S(1)}, f32[768,1,8,128]{0,3,2,1:T(8,128)})) conditional(s32[]{:T(128)} %convert_element_type.37, (f32[768,1,8]{0,2,1:T(8,128)S(1)}, f32[768,1,8]{0,2,1:T(8,128)S(1)}, f32[768,1,8,128]{0,3,2,1:T(8,128)}) %tuple.77, (s32[]{:T(128)}, s32[]{:T(128)}, s32[768]{0:T(1024)S(1)}, ...), branch_computations={%region_5.5_spmd, %region_6.8_spmd} | conditional | flops 2480623104 | bytes 143149152 | solution.py:51
  265.8 8.1 %bitcast_add_fusion = f32[768,1,8,128]{0,3,2,1:T(8,128)} fusion(f32[768,1,8,128]{0,3,2,1:T(8,128)} %get-tuple-element.441, f32[768,768,8]{1,0,2:T(8,128)S(1)} %get-tuple-element.562, f32[768,8]{0,1:T(8,128)S(1)} %bitcast.85, pred[768,768]{0,1:T(8,128)(4,1)S(1)} %compare_and_fusion, f32[768,8]{0,1:T(8,128)S(1)} %get-tuple-element.559, ...), kind=kOutput, calls=%fused_computation.9 | convolution fusion | flops 1233125376 | bytes 26001412 | tf_op jit(solution)/shard_map/while/body/eval_jaxpr/cond/branch_1_fun/qhgk,khd->qhgd/dot_general | solution.py:37
  273.9 10.9 %fusion.4 = f32[768,8]{0,1:T(8,128)S(1)} fusion(f32[768,768,8]{1,0,2:T(8,128)} %copy-done.1, f32[768,8]{0,1:T(8,128)S(1)} %bitcast.86, pred[768,768]{0,1:T(8,128)(4,1)S(1)} %compare_and_fusion), kind=kLoop, calls=%fused_computation.5 | loop fusion | flops 23586816 | bytes 19513344 | tf_op jit(solution)/shard_map/while/body/eval_jaxpr/cond/branch_1_fun/reduce_sum | solution.py:36
  286.1 30.2 %conditional.3 = ((f32[768,1,8]{0,2,1:T(8,128)S(1)}, f32[768,1,8]{0,2,1:T(8,128)S(1)}, f32[768,1,8,128]{0,3,2,1:T(8,128)})) conditional(s32[]{:T(128)} %convert_element_type.37, (f32[768,1,8]{0,2,1:T(8,128)S(1)}, f32[768,1,8]{0,2,1:T(8,128)S(1)}, f32[768,1,8,128]{0,3,2,1:T(8,128)}) %tuple.77, (s32[]{:T(128)}, s32[]{:T(128)}, s32[768]{0:T(1024)S(1)}, ...), branch_computations={%region_5.5_spmd, %region_6.8_spmd} | conditional | flops 2480623104 | bytes 143149152 | solution.py:51
  297.2 8.1 %bitcast_add_fusion = f32[768,1,8,128]{0,3,2,1:T(8,128)} fusion(f32[768,1,8,128]{0,3,2,1:T(8,128)} %get-tuple-element.441, f32[768,768,8]{1,0,2:T(8,128)S(1)} %get-tuple-element.562, f32[768,8]{0,1:T(8,128)S(1)} %bitcast.85, pred[768,768]{0,1:T(8,128)(4,1)S(1)} %compare_and_fusion, f32[768,8]{0,1:T(8,128)S(1)} %get-tuple-element.559, ...), kind=kOutput, calls=%fused_computation.9 | convolution fusion | flops 1233125376 | bytes 26001412 | tf_op jit(solution)/shard_map/while/body/eval_jaxpr/cond/branch_1_fun/qhgk,khd->qhgd/dot_general | solution.py:37
  305.3 10.9 %fusion.4 = f32[768,8]{0,1:T(8,128)S(1)} fusion(f32[768,768,8]{1,0,2:T(8,128)} %copy-done.1, f32[768,8]{0,1:T(8,128)S(1)} %bitcast.86, pred[768,768]{0,1:T(8,128)(4,1)S(1)} %compare_and_fusion), kind=kLoop, calls=%fused_computation.5 | loop fusion | flops 23586816 | bytes 19513344 | tf_op jit(solution)/shard_map/while/body/eval_jaxpr/cond/branch_1_fun/reduce_sum | solution.py:36
  317.5 30.2 %conditional.3 = ((f32[768,1,8]{0,2,1:T(8,128)S(1)}, f32[768,1,8]{0,2,1:T(8,128)S(1)}, f32[768,1,8,128]{0,3,2,1:T(8,128)})) conditional(s32[]{:T(128)} %convert_element_type.37, (f32[768,1,8]{0,2,1:T(8,128)S(1)}, f32[768,1,8]{0,2,1:T(8,128)S(1)}, f32[768,1,8,128]{0,3,2,1:T(8,128)}) %tuple.77, (s32[]{:T(128)}, s32[]{:T(128)}, s32[768]{0:T(1024)S(1)}, ...), branch_computations={%region_5.5_spmd, %region_6.8_spmd} | conditional | flops 2480623104 | bytes 143149152 | solution.py:51
  328.6 8.1 %bitcast_add_fusion = f32[768,1,8,128]{0,3,2,1:T(8,128)} fusion(f32[768,1,8,128]{0,3,2,1:T(8,128)} %get-tuple-element.441, f32[768,768,8]{1,0,2:T(8,128)S(1)} %get-tuple-element.562, f32[768,8]{0,1:T(8,128)S(1)} %bitcast.85, pred[768,768]{0,1:T(8,128)(4,1)S(1)} %compare_and_fusion, f32[768,8]{0,1:T(8,128)S(1)} %get-tuple-element.559, ...), kind=kOutput, calls=%fused_computation.9 | convolution fusion | flops 1233125376 | bytes 26001412 | tf_op jit(solution)/shard_map/while/body/eval_jaxpr/cond/branch_1_fun/qhgk,khd->qhgd/dot_general | solution.py:37
  336.7 10.9 %fusion.4 = f32[768,8]{0,1:T(8,128)S(1)} fusion(f32[768,768,8]{1,0,2:T(8,128)} %copy-done.1, f32[768,8]{0,1:T(8,128)S(1)} %bitcast.86, pred[768,768]{0,1:T(8,128)(4,1)S(1)} %compare_and_fusion), kind=kLoop, calls=%fused_computation.5 | loop fusion | flops 23586816 | bytes 19513344 | tf_op jit(solution)/shard_map/while/body/eval_jaxpr/cond/branch_1_fun/reduce_sum | solution.py:36
  348.9 30.2 %conditional.3 = ((f32[768,1,8]{0,2,1:T(8,128)S(1)}, f32[768,1,8]{0,2,1:T(8,128)S(1)}, f32[768,1,8,128]{0,3,2,1:T(8,128)})) conditional(s32[]{:T(128)} %convert_element_type.37, (f32[768,1,8]{0,2,1:T(8,128)S(1)}, f32[768,1,8]{0,2,1:T(8,128)S(1)}, f32[768,1,8,128]{0,3,2,1:T(8,128)}) %tuple.77, (s32[]{:T(128)}, s32[]{:T(128)}, s32[768]{0:T(1024)S(1)}, ...), branch_computations={%region_5.5_spmd, %region_6.8_spmd} | conditional | flops 2480623104 | bytes 143149152 | solution.py:51
  360.0 8.1 %bitcast_add_fusion = f32[768,1,8,128]{0,3,2,1:T(8,128)} fusion(f32[768,1,8,128]{0,3,2,1:T(8,128)} %get-tuple-element.441, f32[768,768,8]{1,0,2:T(8,128)S(1)} %get-tuple-element.562, f32[768,8]{0,1:T(8,128)S(1)} %bitcast.85, pred[768,768]{0,1:T(8,128)(4,1)S(1)} %compare_and_fusion, f32[768,8]{0,1:T(8,128)S(1)} %get-tuple-element.559, ...), kind=kOutput, calls=%fused_computation.9 | convolution fusion | flops 1233125376 | bytes 26001412 | tf_op jit(solution)/shard_map/while/body/eval_jaxpr/cond/branch_1_fun/qhgk,khd->qhgd/dot_general | solution.py:37
  368.1 10.9 %fusion.4 = f32[768,8]{0,1:T(8,128)S(1)} fusion(f32[768,768,8]{1,0,2:T(8,128)} %copy-done.1, f32[768,8]{0,1:T(8,128)S(1)} %bitcast.86, pred[768,768]{0,1:T(8,128)(4,1)S(1)} %compare_and_fusion), kind=kLoop, calls=%fused_computation.5 | loop fusion | flops 23586816 | bytes 19513344 | tf_op jit(solution)/shard_map/while/body/eval_jaxpr/cond/branch_1_fun/reduce_sum | solution.py:36
  380.3 30.2 %conditional.3 = ((f32[768,1,8]{0,2,1:T(8,128)S(1)}, f32[768,1,8]{0,2,1:T(8,128)S(1)}, f32[768,1,8,128]{0,3,2,1:T(8,128)})) conditional(s32[]{:T(128)} %convert_element_type.37, (f32[768,1,8]{0,2,1:T(8,128)S(1)}, f32[768,1,8]{0,2,1:T(8,128)S(1)}, f32[768,1,8,128]{0,3,2,1:T(8,128)}) %tuple.77, (s32[]{:T(128)}, s32[]{:T(128)}, s32[768]{0:T(1024)S(1)}, ...), branch_computations={%region_5.5_spmd, %region_6.8_spmd} | conditional | flops 2480623104 | bytes 143149152 | solution.py:51
  391.4 8.1 %bitcast_add_fusion = f32[768,1,8,128]{0,3,2,1:T(8,128)} fusion(f32[768,1,8,128]{0,3,2,1:T(8,128)} %get-tuple-element.441, f32[768,768,8]{1,0,2:T(8,128)S(1)} %get-tuple-element.562, f32[768,8]{0,1:T(8,128)S(1)} %bitcast.85, pred[768,768]{0,1:T(8,128)(4,1)S(1)} %compare_and_fusion, f32[768,8]{0,1:T(8,128)S(1)} %get-tuple-element.559, ...), kind=kOutput, calls=%fused_computation.9 | convolution fusion | flops 1233125376 | bytes 26001412 | tf_op jit(solution)/shard_map/while/body/eval_jaxpr/cond/branch_1_fun/qhgk,khd->qhgd/dot_general | solution.py:37
  399.5 10.9 %fusion.4 = f32[768,8]{0,1:T(8,128)S(1)} fusion(f32[768,768,8]{1,0,2:T(8,128)} %copy-done.1, f32[768,8]{0,1:T(8,128)S(1)} %bitcast.86, pred[768,768]{0,1:T(8,128)(4,1)S(1)} %compare_and_fusion), kind=kLoop, calls=%fused_computation.5 | loop fusion | flops 23586816 | bytes 19513344 | tf_op jit(solution)/shard_map/while/body/eval_jaxpr/cond/branch_1_fun/reduce_sum | solution.py:36
  411.7 30.2 %conditional.3 = ((f32[768,1,8]{0,2,1:T(8,128)S(1)}, f32[768,1,8]{0,2,1:T(8,128)S(1)}, f32[768,1,8,128]{0,3,2,1:T(8,128)})) conditional(s32[]{:T(128)} %convert_element_type.37, (f32[768,1,8]{0,2,1:T(8,128)S(1)}, f32[768,1,8]{0,2,1:T(8,128)S(1)}, f32[768,1,8,128]{0,3,2,1:T(8,128)}) %tuple.77, (s32[]{:T(128)}, s32[]{:T(128)}, s32[768]{0:T(1024)S(1)}, ...), branch_computations={%region_5.5_spmd, %region_6.8_spmd} | conditional | flops 2480623104 | bytes 143149152 | solution.py:51
  422.8 8.1 %bitcast_add_fusion = f32[768,1,8,128]{0,3,2,1:T(8,128)} fusion(f32[768,1,8,128]{0,3,2,1:T(8,128)} %get-tuple-element.441, f32[768,768,8]{1,0,2:T(8,128)S(1)} %get-tuple-element.562, f32[768,8]{0,1:T(8,128)S(1)} %bitcast.85, pred[768,768]{0,1:T(8,128)(4,1)S(1)} %compare_and_fusion, f32[768,8]{0,1:T(8,128)S(1)} %get-tuple-element.559, ...), kind=kOutput, calls=%fused_computation.9 | convolution fusion | flops 1233125376 | bytes 26001412 | tf_op jit(solution)/shard_map/while/body/eval_jaxpr/cond/branch_1_fun/qhgk,khd->qhgd/dot_general | solution.py:37
  430.9 10.9 %fusion.4 = f32[768,8]{0,1:T(8,128)S(1)} fusion(f32[768,768,8]{1,0,2:T(8,128)} %copy-done.1, f32[768,8]{0,1:T(8,128)S(1)} %bitcast.86, pred[768,768]{0,1:T(8,128)(4,1)S(1)} %compare_and_fusion), kind=kLoop, calls=%fused_computation.5 | loop fusion | flops 23586816 | bytes 19513344 | tf_op jit(solution)/shard_map/while/body/eval_jaxpr/cond/branch_1_fun/reduce_sum | solution.py:36
  443.1 30.2 %conditional.3 = ((f32[768,1,8]{0,2,1:T(8,128)S(1)}, f32[768,1,8]{0,2,1:T(8,128)S(1)}, f32[768,1,8,128]{0,3,2,1:T(8,128)})) conditional(s32[]{:T(128)} %convert_element_type.37, (f32[768,1,8]{0,2,1:T(8,128)S(1)}, f32[768,1,8]{0,2,1:T(8,128)S(1)}, f32[768,1,8,128]{0,3,2,1:T(8,128)}) %tuple.77, (s32[]{:T(128)}, s32[]{:T(128)}, s32[768]{0:T(1024)S(1)}, ...), branch_computations={%region_5.5_spmd, %region_6.8_spmd} | conditional | flops 2480623104 | bytes 143149152 | solution.py:51
  462.3 10.9 %fusion.4 = f32[768,8]{0,1:T(8,128)S(1)} fusion(f32[768,768,8]{1,0,2:T(8,128)} %copy-done.1, f32[768,8]{0,1:T(8,128)S(1)} %bitcast.86, pred[768,768]{0,1:T(8,128)(4,1)S(1)} %compare_and_fusion), kind=kLoop, calls=%fused_computation.5 | loop fusion | flops 23586816 | bytes 19513344 | tf_op jit(solution)/shard_map/while/body/eval_jaxpr/cond/branch_1_fun/reduce_sum | solution.py:36
  474.5 30.2 %conditional.3 = ((f32[768,1,8]{0,2,1:T(8,128)S(1)}, f32[768,1,8]{0,2,1:T(8,128)S(1)}, f32[768,1,8,128]{0,3,2,1:T(8,128)})) conditional(s32[]{:T(128)} %convert_element_type.37, (f32[768,1,8]{0,2,1:T(8,128)S(1)}, f32[768,1,8]{0,2,1:T(8,128)S(1)}, f32[768,1,8,128]{0,3,2,1:T(8,128)}) %tuple.77, (s32[]{:T(128)}, s32[]{:T(128)}, s32[768]{0:T(1024)S(1)}, ...), branch_computations={%region_5.5_spmd, %region_6.8_spmd} | conditional | flops 2480623104 | bytes 143149152 | solution.py:51
  493.7 10.9 %fusion.4 = f32[768,8]{0,1:T(8,128)S(1)} fusion(f32[768,768,8]{1,0,2:T(8,128)} %copy-done.1, f32[768,8]{0,1:T(8,128)S(1)} %bitcast.86, pred[768,768]{0,1:T(8,128)(4,1)S(1)} %compare_and_fusion), kind=kLoop, calls=%fused_computation.5 | loop fusion | flops 23586816 | bytes 19513344 | tf_op jit(solution)/shard_map/while/body/eval_jaxpr/cond/branch_1_fun/reduce_sum | solution.py:36
  505.9 30.2 %conditional.3 = ((f32[768,1,8]{0,2,1:T(8,128)S(1)}, f32[768,1,8]{0,2,1:T(8,128)S(1)}, f32[768,1,8,128]{0,3,2,1:T(8,128)})) conditional(s32[]{:T(128)} %convert_element_type.37, (f32[768,1,8]{0,2,1:T(8,128)S(1)}, f32[768,1,8]{0,2,1:T(8,128)S(1)}, f32[768,1,8,128]{0,3,2,1:T(8,128)}) %tuple.77, (s32[]{:T(128)}, s32[]{:T(128)}, s32[768]{0:T(1024)S(1)}, ...), branch_computations={%region_5.5_spmd, %region_6.8_spmd} | conditional | flops 2480623104 | bytes 143149152 | solution.py:51
  525.0 10.9 %fusion.4 = f32[768,8]{0,1:T(8,128)S(1)} fusion(f32[768,768,8]{1,0,2:T(8,128)} %copy-done.1, f32[768,8]{0,1:T(8,128)S(1)} %bitcast.86, pred[768,768]{0,1:T(8,128)(4,1)S(1)} %compare_and_fusion), kind=kLoop, calls=%fused_computation.5 | loop fusion | flops 23586816 | bytes 19513344 | tf_op jit(solution)/shard_map/while/body/eval_jaxpr/cond/branch_1_fun/reduce_sum | solution.py:36
  537.2 30.2 %conditional.3 = ((f32[768,1,8]{0,2,1:T(8,128)S(1)}, f32[768,1,8]{0,2,1:T(8,128)S(1)}, f32[768,1,8,128]{0,3,2,1:T(8,128)})) conditional(s32[]{:T(128)} %convert_element_type.37, (f32[768,1,8]{0,2,1:T(8,128)S(1)}, f32[768,1,8]{0,2,1:T(8,128)S(1)}, f32[768,1,8,128]{0,3,2,1:T(8,128)}) %tuple.77, (s32[]{:T(128)}, s32[]{:T(128)}, s32[768]{0:T(1024)S(1)}, ...), branch_computations={%region_5.5_spmd, %region_6.8_spmd} | conditional | flops 2480623104 | bytes 143149152 | solution.py:51
  556.4 10.9 %fusion.4 = f32[768,8]{0,1:T(8,128)S(1)} fusion(f32[768,768,8]{1,0,2:T(8,128)} %copy-done.1, f32[768,8]{0,1:T(8,128)S(1)} %bitcast.86, pred[768,768]{0,1:T(8,128)(4,1)S(1)} %compare_and_fusion), kind=kLoop, calls=%fused_computation.5 | loop fusion | flops 23586816 | bytes 19513344 | tf_op jit(solution)/shard_map/while/body/eval_jaxpr/cond/branch_1_fun/reduce_sum | solution.py:36
  568.6 30.2 %conditional.3 = ((f32[768,1,8]{0,2,1:T(8,128)S(1)}, f32[768,1,8]{0,2,1:T(8,128)S(1)}, f32[768,1,8,128]{0,3,2,1:T(8,128)})) conditional(s32[]{:T(128)} %convert_element_type.37, (f32[768,1,8]{0,2,1:T(8,128)S(1)}, f32[768,1,8]{0,2,1:T(8,128)S(1)}, f32[768,1,8,128]{0,3,2,1:T(8,128)}) %tuple.77, (s32[]{:T(128)}, s32[]{:T(128)}, s32[768]{0:T(1024)S(1)}, ...), branch_computations={%region_5.5_spmd, %region_6.8_spmd} | conditional | flops 2480623104 | bytes 143149152 | solution.py:51
  587.8 10.9 %fusion.4 = f32[768,8]{0,1:T(8,128)S(1)} fusion(f32[768,768,8]{1,0,2:T(8,128)} %copy-done.1, f32[768,8]{0,1:T(8,128)S(1)} %bitcast.86, pred[768,768]{0,1:T(8,128)(4,1)S(1)} %compare_and_fusion), kind=kLoop, calls=%fused_computation.5 | loop fusion | flops 23586816 | bytes 19513344 | tf_op jit(solution)/shard_map/while/body/eval_jaxpr/cond/branch_1_fun/reduce_sum | solution.py:36
  600.0 30.2 %conditional.3 = ((f32[768,1,8]{0,2,1:T(8,128)S(1)}, f32[768,1,8]{0,2,1:T(8,128)S(1)}, f32[768,1,8,128]{0,3,2,1:T(8,128)})) conditional(s32[]{:T(128)} %convert_element_type.37, (f32[768,1,8]{0,2,1:T(8,128)S(1)}, f32[768,1,8]{0,2,1:T(8,128)S(1)}, f32[768,1,8,128]{0,3,2,1:T(8,128)}) %tuple.77, (s32[]{:T(128)}, s32[]{:T(128)}, s32[768]{0:T(1024)S(1)}, ...), branch_computations={%region_5.5_spmd, %region_6.8_spmd} | conditional | flops 2480623104 | bytes 143149152 | solution.py:51
  619.2 10.9 %fusion.4 = f32[768,8]{0,1:T(8,128)S(1)} fusion(f32[768,768,8]{1,0,2:T(8,128)} %copy-done.1, f32[768,8]{0,1:T(8,128)S(1)} %bitcast.86, pred[768,768]{0,1:T(8,128)(4,1)S(1)} %compare_and_fusion), kind=kLoop, calls=%fused_computation.5 | loop fusion | flops 23586816 | bytes 19513344 | tf_op jit(solution)/shard_map/while/body/eval_jaxpr/cond/branch_1_fun/reduce_sum | solution.py:36
  631.4 30.2 %conditional.3 = ((f32[768,1,8]{0,2,1:T(8,128)S(1)}, f32[768,1,8]{0,2,1:T(8,128)S(1)}, f32[768,1,8,128]{0,3,2,1:T(8,128)})) conditional(s32[]{:T(128)} %convert_element_type.37, (f32[768,1,8]{0,2,1:T(8,128)S(1)}, f32[768,1,8]{0,2,1:T(8,128)S(1)}, f32[768,1,8,128]{0,3,2,1:T(8,128)}) %tuple.77, (s32[]{:T(128)}, s32[]{:T(128)}, s32[768]{0:T(1024)S(1)}, ...), branch_computations={%region_5.5_spmd, %region_6.8_spmd} | conditional | flops 2480623104 | bytes 143149152 | solution.py:51
  650.6 10.9 %fusion.4 = f32[768,8]{0,1:T(8,128)S(1)} fusion(f32[768,768,8]{1,0,2:T(8,128)} %copy-done.1, f32[768,8]{0,1:T(8,128)S(1)} %bitcast.86, pred[768,768]{0,1:T(8,128)(4,1)S(1)} %compare_and_fusion), kind=kLoop, calls=%fused_computation.5 | loop fusion | flops 23586816 | bytes 19513344 | tf_op jit(solution)/shard_map/while/body/eval_jaxpr/cond/branch_1_fun/reduce_sum | solution.py:36
  662.8 30.2 %conditional.3 = ((f32[768,1,8]{0,2,1:T(8,128)S(1)}, f32[768,1,8]{0,2,1:T(8,128)S(1)}, f32[768,1,8,128]{0,3,2,1:T(8,128)})) conditional(s32[]{:T(128)} %convert_element_type.37, (f32[768,1,8]{0,2,1:T(8,128)S(1)}, f32[768,1,8]{0,2,1:T(8,128)S(1)}, f32[768,1,8,128]{0,3,2,1:T(8,128)}) %tuple.77, (s32[]{:T(128)}, s32[]{:T(128)}, s32[768]{0:T(1024)S(1)}, ...), branch_computations={%region_5.5_spmd, %region_6.8_spmd} | conditional | flops 2480623104 | bytes 143149152 | solution.py:51
  682.0 10.9 %fusion.4 = f32[768,8]{0,1:T(8,128)S(1)} fusion(f32[768,768,8]{1,0,2:T(8,128)} %copy-done.1, f32[768,8]{0,1:T(8,128)S(1)} %bitcast.86, pred[768,768]{0,1:T(8,128)(4,1)S(1)} %compare_and_fusion), kind=kLoop, calls=%fused_computation.5 | loop fusion | flops 23586816 | bytes 19513344 | tf_op jit(solution)/shard_map/while/body/eval_jaxpr/cond/branch_1_fun/reduce_sum | solution.py:36
  694.2 30.2 %conditional.3 = ((f32[768,1,8]{0,2,1:T(8,128)S(1)}, f32[768,1,8]{0,2,1:T(8,128)S(1)}, f32[768,1,8,128]{0,3,2,1:T(8,128)})) conditional(s32[]{:T(128)} %convert_element_type.37, (f32[768,1,8]{0,2,1:T(8,128)S(1)}, f32[768,1,8]{0,2,1:T(8,128)S(1)}, f32[768,1,8,128]{0,3,2,1:T(8,128)}) %tuple.77, (s32[]{:T(128)}, s32[]{:T(128)}, s32[768]{0:T(1024)S(1)}, ...), branch_computations={%region_5.5_spmd, %region_6.8_spmd} | conditional | flops 2480623104 | bytes 143149152 | solution.py:51
  713.4 10.9 %fusion.4 = f32[768,8]{0,1:T(8,128)S(1)} fusion(f32[768,768,8]{1,0,2:T(8,128)} %copy-done.1, f32[768,8]{0,1:T(8,128)S(1)} %bitcast.86, pred[768,768]{0,1:T(8,128)(4,1)S(1)} %compare_and_fusion), kind=kLoop, calls=%fused_computation.5 | loop fusion | flops 23586816 | bytes 19513344 | tf_op jit(solution)/shard_map/while/body/eval_jaxpr/cond/branch_1_fun/reduce_sum | solution.py:36
  725.6 30.2 %conditional.3 = ((f32[768,1,8]{0,2,1:T(8,128)S(1)}, f32[768,1,8]{0,2,1:T(8,128)S(1)}, f32[768,1,8,128]{0,3,2,1:T(8,128)})) conditional(s32[]{:T(128)} %convert_element_type.37, (f32[768,1,8]{0,2,1:T(8,128)S(1)}, f32[768,1,8]{0,2,1:T(8,128)S(1)}, f32[768,1,8,128]{0,3,2,1:T(8,128)}) %tuple.77, (s32[]{:T(128)}, s32[]{:T(128)}, s32[768]{0:T(1024)S(1)}, ...), branch_computations={%region_5.5_spmd, %region_6.8_spmd} | conditional | flops 2480623104 | bytes 143149152 | solution.py:51
  744.8 10.9 %fusion.4 = f32[768,8]{0,1:T(8,128)S(1)} fusion(f32[768,768,8]{1,0,2:T(8,128)} %copy-done.1, f32[768,8]{0,1:T(8,128)S(1)} %bitcast.86, pred[768,768]{0,1:T(8,128)(4,1)S(1)} %compare_and_fusion), kind=kLoop, calls=%fused_computation.5 | loop fusion | flops 23586816 | bytes 19513344 | tf_op jit(solution)/shard_map/while/body/eval_jaxpr/cond/branch_1_fun/reduce_sum | solution.py:36
  768.6 19.6 %all_to_all.66 = bf16[8,96,1024]{2,1,0:T(8,128)(2,1)S(1)} all-to-all(bf16[8,96,1024]{2,1,0:T(8,128)(2,1)S(1)} %convert_element_type.27), channel_id=1, replica_groups=mesh['dp'=32,'head'=8] {'head'}, dimensions={0} | all-to-all | bytes 3145728 | tf_op jit(solution)/shard_map/all_to_all | solution.py:99
  (220 shorter events, 295.3 us)
Async XLA Ops:
  6.5 0.9 copy-start
  6.5 30.4 %copy-start.2 = (s32[8]{0:T(128)S(1)}, s32[8]{0:T(128)}, u32[]{:S(2)}) copy-start(s32[8]{0:T(128)} %param.11) | copy-start | bytes 100
  6.5 110.4 %all-gather.5.cloned.1.call-start = ((), (), s32[]{:S(2)}) async-start(), calls=%async_computation.5 | async-start | bytes 6488064 | tf_op jit(solution)/shard_map/all_gather | solution.py:82
  19.1 191.0 %all-gather.3.cloned.1.call-start = ((), (), s32[]{:S(2)}) async-start(), calls=%async_computation.4 | async-start | bytes 6488064 | tf_op jit(solution)/shard_map/all_gather | solution.py:81
  32.7 23.7 %all-to-all-start.1 = ((bf16[96,8,1024]{2,0,1:T(8,128)(2,1)}), bf16[96,8,1024]{2,0,1:T(8,128)(2,1)S(1)}, u32[]{:S(2)}, u32[]{:S(2)}) async-start(bf16[96,8,1024]{2,0,1:T(8,128)(2,1)} %bitcast.84), calls=%async_computation.1 | async-start | bytes 3145728 | tf_op jit(solution)/shard_map/all_to_all | solution.py:61
  228.0 6.5 copy-start.1
  259.4 6.5 copy-start.1
  290.8 6.5 copy-start.1
  322.2 6.5 copy-start.1
  353.6 6.5 copy-start.1
  384.9 6.5 copy-start.1
  416.3 6.5 copy-start.1
  447.7 6.5 copy-start.1
  479.1 6.5 copy-start.1
  510.5 6.5 copy-start.1
  541.9 6.5 copy-start.1
  573.3 6.5 copy-start.1
  604.7 6.5 copy-start.1
  636.1 6.5 copy-start.1
  667.5 6.5 copy-start.1
  698.9 6.5 copy-start.1
  730.3 6.5 copy-start.1
Sparse Core Ops, SparseCore 0:
  19.2 97.6 all-gather.4
  119.7 90.3 all-gather.2
where the time goes:
time: 799 us; the launch traced here: 796 us
  matrix products  207 us (26%)
  other arithmetic  199 us (25%)
  waiting for transfers between devices  163 us (20%)
  local copies, waits for them, and re-layouts  129 us (16%)
  loops' own time  41.2 us (5%)
  blocking collectives  40.9 us (5%)
  between operations  13.5 us (2%)
    reduce_sum x17, other arithmetic, attend_block(): totals = totals * factor + jnp.sum(weights, axis=3)  186 us
    dot_general x17, matrix products, attend_block(): jnp.einsum('qhgk,khd->qhgd', weights.astype(jnp.bfloat16), value_block, p...  137 us
    cond x51, local copies, waits for them, and re-layouts  110 us
    all_gather x1, waiting for transfers between devices, on_device(): key_piece = lax.all_gather(key_heads, 'dp', axis=0, tiled=True)  84.5 us
    dot_general x17, matrix products, attend_block(): jnp.einsum('qhgd,khd->qhgk', query_rows, key_block, preferred_element_typ...  69.6 us
    all_gather x1, waiting for transfers between devices, on_device(): value_piece = lax.all_gather(value_heads, 'dp', axis=0, tiled=True)  60 us
    another operation x1, loops' own time, on_device(): lax.fori_loop(0, key_piece.shape[0] // block_width, fold_step, state)  39.5 us
    all_to_all x1, blocking collectives, on_device(): lax.all_to_all(attended, 'head', split_axis=0, concat_axis=1, tiled=True)  19.6 us
  transfers between devices with their start and end apart: 3, of which 3 were waited for; matrix products, arithmetic and copies ran while one was open for 2% of the time, Pallas kernels for 0%

commit v1 on v0

--- a/solution.py
+++ b/solution.py
@@ -78,8 +78,9 @@
         jnp.zeros((set_rows, local_kv, group_heads), jnp.float32),
         jnp.zeros((set_rows, local_kv, group_heads, DH), jnp.float32),
     )
-    key_piece = lax.all_gather(key_heads, "dp", axis=0, tiled=True)
-    value_piece = lax.all_gather(value_heads, "dp", axis=0, tiled=True)
+    val2 = jnp.concatenate([key_heads, value_heads], axis=1)
+    long_array = lax.all_gather(val2, "dp", axis=0, tiled=True)
+    key_piece, value_piece = jnp.split(long_array, [key_heads.shape[1]], 1)
     block_width = min(shard_rows, key_piece.shape[0])
 
     def fold_step(number, inner_state):

time: 799 us -> 761 us (0.952)
  waiting for transfers between devices: 163 us -> 118 us
  local copies, waits for them, and re-layouts: 129 us -> 142 us
  blocking collectives: 40.9 us -> 29.2 us
    all_gather x2 -> x1, waiting for transfers between devices: 144 us -> 93.6 us  [on_device(): long_array = lax.all_gather(val2, 'dp', axis=0, tiled=True)]
    split x0 -> x1, local copies, waits for them, and re-layouts: none -> 10.1 us  [on_device(): key_piece, value_piece = jnp.split(long_array, [key_heads.shape[1]], 1)]
    all_to_all x1 -> x0, blocking collectives: 9.75 us -> none  [on_device(): lax.all_to_all(key_states, 'head', split_axis=1, concat_axis=0, tiled=True)]
  transfers between devices with their start and end apart: 3 -> 3, of which waited for: 3 -> 3; matrix products, arithmetic and copies ran while one was open for 2% -> 1% of each run, Pallas kernels for 0% -> 0%
where the time goes in v1:
time: 761 us; the launch traced here: 758 us
  matrix products  207 us (27%)
  other arithmetic  201 us (26%)
  local copies, waits for them, and re-layouts  142 us (19%)
  waiting for transfers between devices  118 us (16%)
  loops' own time  40.1 us (5%)
  blocking collectives  29.2 us (4%)
  between operations  13.5 us (2%)
  starting transfers between devices  8.64 us (1%)
    reduce_sum x17, other arithmetic, attend_block(): totals = totals * factor + jnp.sum(weights, axis=3)  186 us
    dot_general x17, matrix products, attend_block(): jnp.einsum('qhgk,khd->qhgd', weights.astype(jnp.bfloat16), value_block, p...  137 us
    cond x51, local copies, waits for them, and re-layouts  109 us
    all_gather x1, waiting for transfers between devices, on_device(): long_array = lax.all_gather(val2, 'dp', axis=0, tiled=True)  93.6 us
    dot_general x17, matrix products, attend_block(): jnp.einsum('qhgd,khd->qhgk', query_rows, key_block, preferred_element_typ...  70.1 us
    another operation x1, loops' own time, on_device(): lax.fori_loop(0, key_piece.shape[0] // block_width, fold_step, state)  38.5 us
    all_to_all x1, blocking collectives, on_device(): lax.all_to_all(attended, 'head', split_axis=0, concat_axis=1, tiled=True)  19.7 us
    all_to_all x1, waiting for transfers between devices, on_device(): lax.all_to_all(queries, 'head', split_axis=1, concat_axis=0, tiled=True)  18.3 us
  transfers between devices with their start and end apart: 3, of which 3 were waited for; matrix products, arithmetic and copies ran while one was open for 1% of the time, Pallas kernels for 0%

profile of v1, /device:TPU:144, one launch (start us, length us, event | category | flops | bytes accessed | tf_op | source)
XLA Modules:
  0.0 758.5 jit_solution(10067797988877403500)
XLA Ops:
  19.9 9.5 %all_to_all.64 = bf16[96,8,128]{2,0,1:T(8,128)(2,1)S(1)} all-to-all(bf16[96,8,128]{2,0,1:T(8,128)(2,1)S(1)} %copy_bitcast_fusion.1), channel_id=1, replica_groups=mesh['dp'=32,'head'=8] {'head'}, dimensions={1} | all-to-all | bytes 393216 | tf_op jit(solution)/shard_map/all_to_all | solution.py:63
  38.0 18.3 %all-to-all-done.2 = bf16[96,8,1024]{2,0,1:T(8,128)(2,1)S(1)} async-done(((bf16[96,8,1024]{2,0,1:T(8,128)(2,1)}), bf16[96,8,1024]{2,0,1:T(8,128)(2,1)S(1)}, u32[]{:S(2)}, u32[]{:S(2)}) %all-to-all-start.2) | async-done | bytes 1572896 | tf_op jit(solution)/shard_map/all_to_all | solution.py:61
  56.9 93.6 %all-gather.2.cloned.1.call-done = bf16[24576,2,128]{2,0,1:T(8,128)(2,1)} async-done(((bf16[768,2,128]{2,0,1:T(8,128)(2,1)}), bf16[24576,2,128]{2,0,1:T(8,128)(2,1)}) %all-gather.2.cloned.1.call-update) | async-done | bytes 12582928 | tf_op jit(solution)/shard_map/all_gather | solution.py:82
  150.5 10.1 %fusion.24 = (bf16[24576,1,128]{2,0,1:T(8,128)(2,1)}, bf16[24576,1,128]{2,0,1:T(8,128)(2,1)}) fusion(bf16[24576,2,128]{2,0,1:T(8,128)(2,1)} %all-gather.2.cloned.1.call-done), kind=kLoop, calls=%fused_computation.36 | loop fusion | bytes 25165824 | tf_op jit(solution)/shard_map/split | solution.py:83
  160.6 8.7 %copy.36 = bf16[24576,1,128]{0,2,1:T(8,128)(2,1)} copy(bf16[24576,1,128]{2,0,1:T(8,128)(2,1)} %get-tuple-element.576) | data formatting | bytes 12582912
  171.2 551.9 %while.22 = (s32[]{:T(128)}, f32[768,1,8]{0,2,1:T(8,128)S(1)}, f32[768,1,8]{0,2,1:T(8,128)S(1)}, f32[768,1,8,128]{0,3,2,1:T(8,128)}, s32[]{:T(128)}, /*index=5*/...) while((s32[]{:T(128)}, f32[768,1,8]{0,2,1:T(8,128)S(1)}, ...), condition=%wide.region_9.10_spmd.clone, body=%wide.region_4.9_spmd.clone.sunk | while | flops 2480623104 | bytes 143152528 | solution.py:92
  182.2 30.2 %conditional.3 = ((f32[768,1,8]{0,2,1:T(8,128)S(1)}, f32[768,1,8]{0,2,1:T(8,128)S(1)}, f32[768,1,8,128]{0,3,2,1:T(8,128)})) conditional(s32[]{:T(128)} %convert_element_type.37, (f32[768,1,8]{0,2,1:T(8,128)S(1)}, f32[768,1,8]{0,2,1:T(8,128)S(1)}, f32[768,1,8,128]{0,3,2,1:T(8,128)}) %tuple.80, (s32[]{:T(128)}, s32[]{:T(128)}, s32[768]{0:T(1024)S(1)}, ...), branch_computations={%region_5.5_spmd, %region_6.8_spmd} | conditional | flops 2480623104 | bytes 143149152 | solution.py:51
  201.4 10.9 %fusion.4 = f32[768,8]{0,1:T(8,128)S(1)} fusion(f32[768,768,8]{1,0,2:T(8,128)} %copy-done.2, f32[768,8]{0,1:T(8,128)S(1)} %bitcast.86, pred[768,768]{0,1:T(8,128)(4,1)S(1)} %compare_and_fusion), kind=kLoop, calls=%fused_computation.5 | loop fusion | flops 23586816 | bytes 19513344 | tf_op jit(solution)/shard_map/while/body/eval_jaxpr/cond/branch_1_fun/reduce_sum | solution.py:36
  213.5 30.2 %conditional.3 = ((f32[768,1,8]{0,2,1:T(8,128)S(1)}, f32[768,1,8]{0,2,1:T(8,128)S(1)}, f32[768,1,8,128]{0,3,2,1:T(8,128)})) conditional(s32[]{:T(128)} %convert_element_type.37, (f32[768,1,8]{0,2,1:T(8,128)S(1)}, f32[768,1,8]{0,2,1:T(8,128)S(1)}, f32[768,1,8,128]{0,3,2,1:T(8,128)}) %tuple.80, (s32[]{:T(128)}, s32[]{:T(128)}, s32[768]{0:T(1024)S(1)}, ...), branch_computations={%region_5.5_spmd, %region_6.8_spmd} | conditional | flops 2480623104 | bytes 143149152 | solution.py:51
  232.7 10.9 %fusion.4 = f32[768,8]{0,1:T(8,128)S(1)} fusion(f32[768,768,8]{1,0,2:T(8,128)} %copy-done.2, f32[768,8]{0,1:T(8,128)S(1)} %bitcast.86, pred[768,768]{0,1:T(8,128)(4,1)S(1)} %compare_and_fusion), kind=kLoop, calls=%fused_computation.5 | loop fusion | flops 23586816 | bytes 19513344 | tf_op jit(solution)/shard_map/while/body/eval_jaxpr/cond/branch_1_fun/reduce_sum | solution.py:36
  244.9 30.2 %conditional.3 = ((f32[768,1,8]{0,2,1:T(8,128)S(1)}, f32[768,1,8]{0,2,1:T(8,128)S(1)}, f32[768,1,8,128]{0,3,2,1:T(8,128)})) conditional(s32[]{:T(128)} %convert_element_type.37, (f32[768,1,8]{0,2,1:T(8,128)S(1)}, f32[768,1,8]{0,2,1:T(8,128)S(1)}, f32[768,1,8,128]{0,3,2,1:T(8,128)}) %tuple.80, (s32[]{:T(128)}, s32[]{:T(128)}, s32[768]{0:T(1024)S(1)}, ...), branch_computations={%region_5.5_spmd, %region_6.8_spmd} | conditional | flops 2480623104 | bytes 143149152 | solution.py:51
  264.1 10.9 %fusion.4 = f32[768,8]{0,1:T(8,128)S(1)} fusion(f32[768,768,8]{1,0,2:T(8,128)} %copy-done.2, f32[768,8]{0,1:T(8,128)S(1)} %bitcast.86, pred[768,768]{0,1:T(8,128)(4,1)S(1)} %compare_and_fusion), kind=kLoop, calls=%fused_computation.5 | loop fusion | flops 23586816 | bytes 19513344 | tf_op jit(solution)/shard_map/while/body/eval_jaxpr/cond/branch_1_fun/reduce_sum | solution.py:36
  276.3 30.2 %conditional.3 = ((f32[768,1,8]{0,2,1:T(8,128)S(1)}, f32[768,1,8]{0,2,1:T(8,128)S(1)}, f32[768,1,8,128]{0,3,2,1:T(8,128)})) conditional(s32[]{:T(128)} %convert_element_type.37, (f32[768,1,8]{0,2,1:T(8,128)S(1)}, f32[768,1,8]{0,2,1:T(8,128)S(1)}, f32[768,1,8,128]{0,3,2,1:T(8,128)}) %tuple.80, (s32[]{:T(128)}, s32[]{:T(128)}, s32[768]{0:T(1024)S(1)}, ...), branch_computations={%region_5.5_spmd, %region_6.8_spmd} | conditional | flops 2480623104 | bytes 143149152 | solution.py:51
  295.5 10.9 %fusion.4 = f32[768,8]{0,1:T(8,128)S(1)} fusion(f32[768,768,8]{1,0,2:T(8,128)} %copy-done.2, f32[768,8]{0,1:T(8,128)S(1)} %bitcast.86, pred[768,768]{0,1:T(8,128)(4,1)S(1)} %compare_and_fusion), kind=kLoop, calls=%fused_computation.5 | loop fusion | flops 23586816 | bytes 19513344 | tf_op jit(solution)/shard_map/while/body/eval_jaxpr/cond/branch_1_fun/reduce_sum | solution.py:36
  307.7 30.2 %conditional.3 = ((f32[768,1,8]{0,2,1:T(8,128)S(1)}, f32[768,1,8]{0,2,1:T(8,128)S(1)}, f32[768,1,8,128]{0,3,2,1:T(8,128)})) conditional(s32[]{:T(128)} %convert_element_type.37, (f32[768,1,8]{0,2,1:T(8,128)S(1)}, f32[768,1,8]{0,2,1:T(8,128)S(1)}, f32[768,1,8,128]{0,3,2,1:T(8,128)}) %tuple.80, (s32[]{:T(128)}, s32[]{:T(128)}, s32[768]{0:T(1024)S(1)}, ...), branch_computations={%region_5.5_spmd, %region_6.8_spmd} | conditional | flops 2480623104 | bytes 143149152 | solution.py:51
  318.8 8.1 %bitcast_add_fusion = f32[768,1,8,128]{0,3,2,1:T(8,128)} fusion(f32[768,1,8,128]{0,3,2,1:T(8,128)} %get-tuple-element.441, f32[768,768,8]{1,0,2:T(8,128)S(1)} %get-tuple-element.573, f32[768,8]{0,1:T(8,128)S(1)} %bitcast.85, pred[768,768]{0,1:T(8,128)(4,1)S(1)} %compare_and_fusion, f32[768,8]{0,1:T(8,128)S(1)} %get-tuple-element.570, ...), kind=kOutput, calls=%fused_computation.9 | convolution fusion | flops 1233125376 | bytes 26001412 | tf_op jit(solution)/shard_map/while/body/eval_jaxpr/cond/branch_1_fun/qhgk,khd->qhgd/dot_general | solution.py:37
  326.9 10.9 %fusion.4 = f32[768,8]{0,1:T(8,128)S(1)} fusion(f32[768,768,8]{1,0,2:T(8,128)} %copy-done.2, f32[768,8]{0,1:T(8,128)S(1)} %bitcast.86, pred[768,768]{0,1:T(8,128)(4,1)S(1)} %compare_and_fusion), kind=kLoop, calls=%fused_computation.5 | loop fusion | flops 23586816 | bytes 19513344 | tf_op jit(solution)/shard_map/while/body/eval_jaxpr/cond/branch_1_fun/reduce_sum | solution.py:36
  339.1 30.2 %conditional.3 = ((f32[768,1,8]{0,2,1:T(8,128)S(1)}, f32[768,1,8]{0,2,1:T(8,128)S(1)}, f32[768,1,8,128]{0,3,2,1:T(8,128)})) conditional(s32[]{:T(128)} %convert_element_type.37, (f32[768,1,8]{0,2,1:T(8,128)S(1)}, f32[768,1,8]{0,2,1:T(8,128)S(1)}, f32[768,1,8,128]{0,3,2,1:T(8,128)}) %tuple.80, (s32[]{:T(128)}, s32[]{:T(128)}, s32[768]{0:T(1024)S(1)}, ...), branch_computations={%region_5.5_spmd, %region_6.8_spmd} | conditional | flops 2480623104 | bytes 143149152 | solution.py:51
  350.2 8.1 %bitcast_add_fusion = f32[768,1,8,128]{0,3,2,1:T(8,128)} fusion(f32[768,1,8,128]{0,3,2,1:T(8,128)} %get-tuple-element.441, f32[768,768,8]{1,0,2:T(8,128)S(1)} %get-tuple-element.573, f32[768,8]{0,1:T(8,128)S(1)} %bitcast.85, pred[768,768]{0,1:T(8,128)(4,1)S(1)} %compare_and_fusion, f32[768,8]{0,1:T(8,128)S(1)} %get-tuple-element.570, ...), kind=kOutput, calls=%fused_computation.9 | convolution fusion | flops 1233125376 | bytes 26001412 | tf_op jit(solution)/shard_map/while/body/eval_jaxpr/cond/branch_1_fun/qhgk,khd->qhgd/dot_general | solution.py:37
  358.3 10.9 %fusion.4 = f32[768,8]{0,1:T(8,128)S(1)} fusion(f32[768,768,8]{1,0,2:T(8,128)} %copy-done.2, f32[768,8]{0,1:T(8,128)S(1)} %bitcast.86, pred[768,768]{0,1:T(8,128)(4,1)S(1)} %compare_and_fusion), kind=kLoop, calls=%fused_computation.5 | loop fusion | flops 23586816 | bytes 19513344 | tf_op jit(solution)/shard_map/while/body/eval_jaxpr/cond/branch_1_fun/reduce_sum | solution.py:36
  370.5 30.2 %conditional.3 = ((f32[768,1,8]{0,2,1:T(8,128)S(1)}, f32[768,1,8]{0,2,1:T(8,128)S(1)}, f32[768,1,8,128]{0,3,2,1:T(8,128)})) conditional(s32[]{:T(128)} %convert_element_type.37, (f32[768,1,8]{0,2,1:T(8,128)S(1)}, f32[768,1,8]{0,2,1:T(8,128)S(1)}, f32[768,1,8,128]{0,3,2,1:T(8,128)}) %tuple.80, (s32[]{:T(128)}, s32[]{:T(128)}, s32[768]{0:T(1024)S(1)}, ...), branch_computations={%region_5.5_spmd, %region_6.8_spmd} | conditional | flops 2480623104 | bytes 143149152 | solution.py:51
  381.6 8.1 %bitcast_add_fusion = f32[768,1,8,128]{0,3,2,1:T(8,128)} fusion(f32[768,1,8,128]{0,3,2,1:T(8,128)} %get-tuple-element.441, f32[768,768,8]{1,0,2:T(8,128)S(1)} %get-tuple-element.573, f32[768,8]{0,1:T(8,128)S(1)} %bitcast.85, pred[768,768]{0,1:T(8,128)(4,1)S(1)} %compare_and_fusion, f32[768,8]{0,1:T(8,128)S(1)} %get-tuple-element.570, ...), kind=kOutput, calls=%fused_computation.9 | convolution fusion | flops 1233125376 | bytes 26001412 | tf_op jit(solution)/shard_map/while/body/eval_jaxpr/cond/branch_1_fun/qhgk,khd->qhgd/dot_general | solution.py:37
  389.7 10.9 %fusion.4 = f32[768,8]{0,1:T(8,128)S(1)} fusion(f32[768,768,8]{1,0,2:T(8,128)} %copy-done.2, f32[768,8]{0,1:T(8,128)S(1)} %bitcast.86, pred[768,768]{0,1:T(8,128)(4,1)S(1)} %compare_and_fusion), kind=kLoop, calls=%fused_computation.5 | loop fusion | flops 23586816 | bytes 19513344 | tf_op jit(solution)/shard_map/while/body/eval_jaxpr/cond/branch_1_fun/reduce_sum | solution.py:36
  401.8 30.2 %conditional.3 = ((f32[768,1,8]{0,2,1:T(8,128)S(1)}, f32[768,1,8]{0,2,1:T(8,128)S(1)}, f32[768,1,8,128]{0,3,2,1:T(8,128)})) conditional(s32[]{:T(128)} %convert_element_type.37, (f32[768,1,8]{0,2,1:T(8,128)S(1)}, f32[768,1,8]{0,2,1:T(8,128)S(1)}, f32[768,1,8,128]{0,3,2,1:T(8,128)}) %tuple.80, (s32[]{:T(128)}, s32[]{:T(128)}, s32[768]{0:T(1024)S(1)}, ...), branch_computations={%region_5.5_spmd, %region_6.8_spmd} | conditional | flops 2480623104 | bytes 143149152 | solution.py:51
  421.1 10.9 %fusion.4 = f32[768,8]{0,1:T(8,128)S(1)} fusion(f32[768,768,8]{1,0,2:T(8,128)} %copy-done.2, f32[768,8]{0,1:T(8,128)S(1)} %bitcast.86, pred[768,768]{0,1:T(8,128)(4,1)S(1)} %compare_and_fusion), kind=kLoop, calls=%fused_computation.5 | loop fusion | flops 23586816 | bytes 19513344 | tf_op jit(solution)/shard_map/while/body/eval_jaxpr/cond/branch_1_fun/reduce_sum | solution.py:36
  433.2 30.2 %conditional.3 = ((f32[768,1,8]{0,2,1:T(8,128)S(1)}, f32[768,1,8]{0,2,1:T(8,128)S(1)}, f32[768,1,8,128]{0,3,2,1:T(8,128)})) conditional(s32[]{:T(128)} %convert_element_type.37, (f32[768,1,8]{0,2,1:T(8,128)S(1)}, f32[768,1,8]{0,2,1:T(8,128)S(1)}, f32[768,1,8,128]{0,3,2,1:T(8,128)}) %tuple.80, (s32[]{:T(128)}, s32[]{:T(128)}, s32[768]{0:T(1024)S(1)}, ...), branch_computations={%region_5.5_spmd, %region_6.8_spmd} | conditional | flops 2480623104 | bytes 143149152 | solution.py:51
  452.4 10.9 %fusion.4 = f32[768,8]{0,1:T(8,128)S(1)} fusion(f32[768,768,8]{1,0,2:T(8,128)} %copy-done.2, f32[768,8]{0,1:T(8,128)S(1)} %bitcast.86, pred[768,768]{0,1:T(8,128)(4,1)S(1)} %compare_and_fusion), kind=kLoop, calls=%fused_computation.5 | loop fusion | flops 23586816 | bytes 19513344 | tf_op jit(solution)/shard_map/while/body/eval_jaxpr/cond/branch_1_fun/reduce_sum | solution.py:36
  464.6 30.2 %conditional.3 = ((f32[768,1,8]{0,2,1:T(8,128)S(1)}, f32[768,1,8]{0,2,1:T(8,128)S(1)}, f32[768,1,8,128]{0,3,2,1:T(8,128)})) conditional(s32[]{:T(128)} %convert_element_type.37, (f32[768,1,8]{0,2,1:T(8,128)S(1)}, f32[768,1,8]{0,2,1:T(8,128)S(1)}, f32[768,1,8,128]{0,3,2,1:T(8,128)}) %tuple.80, (s32[]{:T(128)}, s32[]{:T(128)}, s32[768]{0:T(1024)S(1)}, ...), branch_computations={%region_5.5_spmd, %region_6.8_spmd} | conditional | flops 2480623104 | bytes 143149152 | solution.py:51
  483.8 10.9 %fusion.4 = f32[768,8]{0,1:T(8,128)S(1)} fusion(f32[768,768,8]{1,0,2:T(8,128)} %copy-done.2, f32[768,8]{0,1:T(8,128)S(1)} %bitcast.86, pred[768,768]{0,1:T(8,128)(4,1)S(1)} %compare_and_fusion), kind=kLoop, calls=%fused_computation.5 | loop fusion | flops 23586816 | bytes 19513344 | tf_op jit(solution)/shard_map/while/body/eval_jaxpr/cond/branch_1_fun/reduce_sum | solution.py:36
  496.0 30.2 %conditional.3 = ((f32[768,1,8]{0,2,1:T(8,128)S(1)}, f32[768,1,8]{0,2,1:T(8,128)S(1)}, f32[768,1,8,128]{0,3,2,1:T(8,128)})) conditional(s32[]{:T(128)} %convert_element_type.37, (f32[768,1,8]{0,2,1:T(8,128)S(1)}, f32[768,1,8]{0,2,1:T(8,128)S(1)}, f32[768,1,8,128]{0,3,2,1:T(8,128)}) %tuple.80, (s32[]{:T(128)}, s32[]{:T(128)}, s32[768]{0:T(1024)S(1)}, ...), branch_computations={%region_5.5_spmd, %region_6.8_spmd} | conditional | flops 2480623104 | bytes 143149152 | solution.py:51
  507.2 8.1 %bitcast_add_fusion = f32[768,1,8,128]{0,3,2,1:T(8,128)} fusion(f32[768,1,8,128]{0,3,2,1:T(8,128)} %get-tuple-element.441, f32[768,768,8]{1,0,2:T(8,128)S(1)} %get-tuple-element.573, f32[768,8]{0,1:T(8,128)S(1)} %bitcast.85, pred[768,768]{0,1:T(8,128)(4,1)S(1)} %compare_and_fusion, f32[768,8]{0,1:T(8,128)S(1)} %get-tuple-element.570, ...), kind=kOutput, calls=%fused_computation.9 | convolution fusion | flops 1233125376 | bytes 26001412 | tf_op jit(solution)/shard_map/while/body/eval_jaxpr/cond/branch_1_fun/qhgk,khd->qhgd/dot_general | solution.py:37
  515.2 10.9 %fusion.4 = f32[768,8]{0,1:T(8,128)S(1)} fusion(f32[768,768,8]{1,0,2:T(8,128)} %copy-done.2, f32[768,8]{0,1:T(8,128)S(1)} %bitcast.86, pred[768,768]{0,1:T(8,128)(4,1)S(1)} %compare_and_fusion), kind=kLoop, calls=%fused_computation.5 | loop fusion | flops 23586816 | bytes 19513344 | tf_op jit(solution)/shard_map/while/body/eval_jaxpr/cond/branch_1_fun/reduce_sum | solution.py:36
  527.4 30.2 %conditional.3 = ((f32[768,1,8]{0,2,1:T(8,128)S(1)}, f32[768,1,8]{0,2,1:T(8,128)S(1)}, f32[768,1,8,128]{0,3,2,1:T(8,128)})) conditional(s32[]{:T(128)} %convert_element_type.37, (f32[768,1,8]{0,2,1:T(8,128)S(1)}, f32[768,1,8]{0,2,1:T(8,128)S(1)}, f32[768,1,8,128]{0,3,2,1:T(8,128)}) %tuple.80, (s32[]{:T(128)}, s32[]{:T(128)}, s32[768]{0:T(1024)S(1)}, ...), branch_computations={%region_5.5_spmd, %region_6.8_spmd} | conditional | flops 2480623104 | bytes 143149152 | solution.py:51
  538.5 8.1 %bitcast_add_fusion = f32[768,1,8,128]{0,3,2,1:T(8,128)} fusion(f32[768,1,8,128]{0,3,2,1:T(8,128)} %get-tuple-element.441, f32[768,768,8]{1,0,2:T(8,128)S(1)} %get-tuple-element.573, f32[768,8]{0,1:T(8,128)S(1)} %bitcast.85, pred[768,768]{0,1:T(8,128)(4,1)S(1)} %compare_and_fusion, f32[768,8]{0,1:T(8,128)S(1)} %get-tuple-element.570, ...), kind=kOutput, calls=%fused_computation.9 | convolution fusion | flops 1233125376 | bytes 26001412 | tf_op jit(solution)/shard_map/while/body/eval_jaxpr/cond/branch_1_fun/qhgk,khd->qhgd/dot_general | solution.py:37
  546.6 10.9 %fusion.4 = f32[768,8]{0,1:T(8,128)S(1)} fusion(f32[768,768,8]{1,0,2:T(8,128)} %copy-done.2, f32[768,8]{0,1:T(8,128)S(1)} %bitcast.86, pred[768,768]{0,1:T(8,128)(4,1)S(1)} %compare_and_fusion), kind=kLoop, calls=%fused_computation.5 | loop fusion | flops 23586816 | bytes 19513344 | tf_op jit(solution)/shard_map/while/body/eval_jaxpr/cond/branch_1_fun/reduce_sum | solution.py:36
  558.8 30.2 %conditional.3 = ((f32[768,1,8]{0,2,1:T(8,128)S(1)}, f32[768,1,8]{0,2,1:T(8,128)S(1)}, f32[768,1,8,128]{0,3,2,1:T(8,128)})) conditional(s32[]{:T(128)} %convert_element_type.37, (f32[768,1,8]{0,2,1:T(8,128)S(1)}, f32[768,1,8]{0,2,1:T(8,128)S(1)}, f32[768,1,8,128]{0,3,2,1:T(8,128)}) %tuple.80, (s32[]{:T(128)}, s32[]{:T(128)}, s32[768]{0:T(1024)S(1)}, ...), branch_computations={%region_5.5_spmd, %region_6.8_spmd} | conditional | flops 2480623104 | bytes 143149152 | solution.py:51
  569.9 8.1 %bitcast_add_fusion = f32[768,1,8,128]{0,3,2,1:T(8,128)} fusion(f32[768,1,8,128]{0,3,2,1:T(8,128)} %get-tuple-element.441, f32[768,768,8]{1,0,2:T(8,128)S(1)} %get-tuple-element.573, f32[768,8]{0,1:T(8,128)S(1)} %bitcast.85, pred[768,768]{0,1:T(8,128)(4,1)S(1)} %compare_and_fusion, f32[768,8]{0,1:T(8,128)S(1)} %get-tuple-element.570, ...), kind=kOutput, calls=%fused_computation.9 | convolution fusion | flops 1233125376 | bytes 26001412 | tf_op jit(solution)/shard_map/while/body/eval_jaxpr/cond/branch_1_fun/qhgk,khd->qhgd/dot_general | solution.py:37
  578.0 10.9 %fusion.4 = f32[768,8]{0,1:T(8,128)S(1)} fusion(f32[768,768,8]{1,0,2:T(8,128)} %copy-done.2, f32[768,8]{0,1:T(8,128)S(1)} %bitcast.86, pred[768,768]{0,1:T(8,128)(4,1)S(1)} %compare_and_fusion), kind=kLoop, calls=%fused_computation.5 | loop fusion | flops 23586816 | bytes 19513344 | tf_op jit(solution)/shard_map/while/body/eval_jaxpr/cond/branch_1_fun/reduce_sum | solution.py:36
  590.1 30.2 %conditional.3 = ((f32[768,1,8]{0,2,1:T(8,128)S(1)}, f32[768,1,8]{0,2,1:T(8,128)S(1)}, f32[768,1,8,128]{0,3,2,1:T(8,128)})) conditional(s32[]{:T(128)} %convert_element_type.37, (f32[768,1,8]{0,2,1:T(8,128)S(1)}, f32[768,1,8]{0,2,1:T(8,128)S(1)}, f32[768,1,8,128]{0,3,2,1:T(8,128)}) %tuple.80, (s32[]{:T(128)}, s32[]{:T(128)}, s32[768]{0:T(1024)S(1)}, ...), branch_computations={%region_5.5_spmd, %region_6.8_spmd} | conditional | flops 2480623104 | bytes 143149152 | solution.py:51
  601.3 8.1 %bitcast_add_fusion = f32[768,1,8,128]{0,3,2,1:T(8,128)} fusion(f32[768,1,8,128]{0,3,2,1:T(8,128)} %get-tuple-element.441, f32[768,768,8]{1,0,2:T(8,128)S(1)} %get-tuple-element.573, f32[768,8]{0,1:T(8,128)S(1)} %bitcast.85, pred[768,768]{0,1:T(8,128)(4,1)S(1)} %compare_and_fusion, f32[768,8]{0,1:T(8,128)S(1)} %get-tuple-element.570, ...), kind=kOutput, calls=%fused_computation.9 | convolution fusion | flops 1233125376 | bytes 26001412 | tf_op jit(solution)/shard_map/while/body/eval_jaxpr/cond/branch_1_fun/qhgk,khd->qhgd/dot_general | solution.py:37
  609.4 10.9 %fusion.4 = f32[768,8]{0,1:T(8,128)S(1)} fusion(f32[768,768,8]{1,0,2:T(8,128)} %copy-done.2, f32[768,8]{0,1:T(8,128)S(1)} %bitcast.86, pred[768,768]{0,1:T(8,128)(4,1)S(1)} %compare_and_fusion), kind=kLoop, calls=%fused_computation.5 | loop fusion | flops 23586816 | bytes 19513344 | tf_op jit(solution)/shard_map/while/body/eval_jaxpr/cond/branch_1_fun/reduce_sum | solution.py:36
  621.5 30.2 %conditional.3 = ((f32[768,1,8]{0,2,1:T(8,128)S(1)}, f32[768,1,8]{0,2,1:T(8,128)S(1)}, f32[768,1,8,128]{0,3,2,1:T(8,128)})) conditional(s32[]{:T(128)} %convert_element_type.37, (f32[768,1,8]{0,2,1:T(8,128)S(1)}, f32[768,1,8]{0,2,1:T(8,128)S(1)}, f32[768,1,8,128]{0,3,2,1:T(8,128)}) %tuple.80, (s32[]{:T(128)}, s32[]{:T(128)}, s32[768]{0:T(1024)S(1)}, ...), branch_computations={%region_5.5_spmd, %region_6.8_spmd} | conditional | flops 2480623104 | bytes 143149152 | solution.py:51
  640.8 10.9 %fusion.4 = f32[768,8]{0,1:T(8,128)S(1)} fusion(f32[768,768,8]{1,0,2:T(8,128)} %copy-done.2, f32[768,8]{0,1:T(8,128)S(1)} %bitcast.86, pred[768,768]{0,1:T(8,128)(4,1)S(1)} %compare_and_fusion), kind=kLoop, calls=%fused_computation.5 | loop fusion | flops 23586816 | bytes 19513344 | tf_op jit(solution)/shard_map/while/body/eval_jaxpr/cond/branch_1_fun/reduce_sum | solution.py:36
  652.9 30.2 %conditional.3 = ((f32[768,1,8]{0,2,1:T(8,128)S(1)}, f32[768,1,8]{0,2,1:T(8,128)S(1)}, f32[768,1,8,128]{0,3,2,1:T(8,128)})) conditional(s32[]{:T(128)} %convert_element_type.37, (f32[768,1,8]{0,2,1:T(8,128)S(1)}, f32[768,1,8]{0,2,1:T(8,128)S(1)}, f32[768,1,8,128]{0,3,2,1:T(8,128)}) %tuple.80, (s32[]{:T(128)}, s32[]{:T(128)}, s32[768]{0:T(1024)S(1)}, ...), branch_computations={%region_5.5_spmd, %region_6.8_spmd} | conditional | flops 2480623104 | bytes 143149152 | solution.py:51
  672.1 10.9 %fusion.4 = f32[768,8]{0,1:T(8,128)S(1)} fusion(f32[768,768,8]{1,0,2:T(8,128)} %copy-done.2, f32[768,8]{0,1:T(8,128)S(1)} %bitcast.86, pred[768,768]{0,1:T(8,128)(4,1)S(1)} %compare_and_fusion), kind=kLoop, calls=%fused_computation.5 | loop fusion | flops 23586816 | bytes 19513344 | tf_op jit(solution)/shard_map/while/body/eval_jaxpr/cond/branch_1_fun/reduce_sum | solution.py:36
  684.3 30.2 %conditional.3 = ((f32[768,1,8]{0,2,1:T(8,128)S(1)}, f32[768,1,8]{0,2,1:T(8,128)S(1)}, f32[768,1,8,128]{0,3,2,1:T(8,128)})) conditional(s32[]{:T(128)} %convert_element_type.37, (f32[768,1,8]{0,2,1:T(8,128)S(1)}, f32[768,1,8]{0,2,1:T(8,128)S(1)}, f32[768,1,8,128]{0,3,2,1:T(8,128)}) %tuple.80, (s32[]{:T(128)}, s32[]{:T(128)}, s32[768]{0:T(1024)S(1)}, ...), branch_computations={%region_5.5_spmd, %region_6.8_spmd} | conditional | flops 2480623104 | bytes 143149152 | solution.py:51
  703.5 10.9 %fusion.4 = f32[768,8]{0,1:T(8,128)S(1)} fusion(f32[768,768,8]{1,0,2:T(8,128)} %copy-done.2, f32[768,8]{0,1:T(8,128)S(1)} %bitcast.86, pred[768,768]{0,1:T(8,128)(4,1)S(1)} %compare_and_fusion), kind=kLoop, calls=%fused_computation.5 | loop fusion | flops 23586816 | bytes 19513344 | tf_op jit(solution)/shard_map/while/body/eval_jaxpr/cond/branch_1_fun/reduce_sum | solution.py:36
  730.6 19.7 %all_to_all.65 = bf16[8,96,1024]{2,1,0:T(8,128)(2,1)S(1)} all-to-all(bf16[8,96,1024]{2,1,0:T(8,128)(2,1)} %convert_element_type.27), channel_id=1, replica_groups=mesh['dp'=32,'head'=8] {'head'}, dimensions={0} | all-to-all | bytes 3145728 | tf_op jit(solution)/shard_map/all_to_all | solution.py:100
  (221 shorter events, 303.1 us)
Async XLA Ops:
  6.5 0.9 copy-start
  7.5 29.0 %copy-start.3 = (s32[8]{0:T(128)S(1)}, s32[8]{0:T(128)}, u32[]{:S(2)}) copy-start(s32[8]{0:T(128)} %param.11) | copy-start | bytes 100
  8.2 11.7 %all-to-all-start = ((bf16[96,8,128]{2,0,1:T(8,128)(2,1)}), bf16[96,8,128]{2,0,1:T(8,128)(2,1)S(1)}, u32[]{:S(2)}, u32[]{:S(2)}) async-start(bf16[96,8,128]{2,0,1:T(8,128)(2,1)} %copy_bitcast_fusion.2), calls=%async_computation | async-start | bytes 393216 | tf_op jit(solution)/shard_map/all_to_all | solution.py:62
  13.2 137.3 %all-gather.2.cloned.1.call-start = ((), (), s32[]{:S(2)}) async-start(), calls=%async_computation.4 | async-start | bytes 12976128 | tf_op jit(solution)/shard_map/all_gather | solution.py:82
  32.9 23.4 %all-to-all-start.2 = ((bf16[96,8,1024]{2,0,1:T(8,128)(2,1)}), bf16[96,8,1024]{2,0,1:T(8,128)(2,1)S(1)}, u32[]{:S(2)}, u32[]{:S(2)}) async-start(bf16[96,8,1024]{2,0,1:T(8,128)(2,1)} %bitcast.84), calls=%async_computation.2 | async-start | bytes 3145728 | tf_op jit(solution)/shard_map/all_to_all | solution.py:61
  186.8 6.5 copy-start.2
  218.2 6.5 copy-start.2
  249.6 6.5 copy-start.2
  281.0 6.5 copy-start.2
  312.4 6.5 copy-start.2
  343.8 6.5 copy-start.2
  375.2 6.5 copy-start.2
  406.5 6.5 copy-start.2
  437.9 6.5 copy-start.2
  469.3 6.5 copy-start.2
  500.7 6.5 copy-start.2
  532.1 6.5 copy-start.2
  563.5 6.5 copy-start.2
  594.9 6.5 copy-start.2
  626.2 6.5 copy-start.2
  657.6 6.5 copy-start.2
  689.0 6.5 copy-start.2
  723.1 28.6 %copy-start.1 = (bf16[96,1024]{1,0:T(8,128)(2,1)S(1)}, bf16[96,1024]{1,0:T(8,128)(2,1)}, u32[]{:S(2)}) copy-start(bf16[96,1024]{1,0:T(8,128)(2,1)} %param.9) | copy-start | bytes 589828
Sparse Core Ops, SparseCore 0:
  30.3 120.2 all-gather.1
